TPU v7x, 128 devices: a whole 4x4x4 slice. The times are simulated.
128 devices in a mesh: dp: 4 (over y_hi, core), feat: 32 (over y_lo, x, z).
Axes of the slice: x: 4, y: 4 (y_hi: 2, y_lo: 2; y = y_hi * 2 + y_lo), z: 4, core: 2. Of those that a mesh axis runs over, the one named last changes fastest.
Arguments:
- tokens: bfloat16 [4096, 65536], P('dp', 'feat'), may hold values from -6 to 6
- left_factor: bfloat16 [256, 256, 256], P('feat'), may hold values from -0.375 to 0.375
- right_factor: bfloat16 [256, 256, 256], P('feat'), may hold values from -0.375 to 0.375
- cotangent: bfloat16 [4096, 65536], P('dp', 'feat'), may hold values from -6 to 6
Outputs:
- output: bfloat16 [4096, 65536], P('dp', 'feat')
- input_grad: bfloat16 [4096, 65536], P('dp', 'feat')
- left_grad: float32 [256, 256, 256], P('feat')
- right_grad: float32 [256, 256, 256], P('feat')
All inputs are finite; a program needn't handle non-finite values.
Results may differ from a plain program's by a relative error of at most 0.0058.
Values may be sent and summed in bfloat16 or wider, within the bound.
A program may use at most 128 MiB of HBM per device.

v0:
```python
import math

import jax
import jax.numpy as jnp
from jax import lax
from jax.sharding import PartitionSpec as P

SQRT_HALF = 0.7071067811865476
INV_ROOT_TWO_PI = 0.3989422804014327


def gelu_exact(value):
    return 0.5 * value * (1.0 + jax.scipy.special.erf(value * SQRT_HALF))


def gelu_slope(value):
    cumulative = 0.5 * (1.0 + jax.scipy.special.erf(value * SQRT_HALF))
    return cumulative + value * jnp.exp(-0.5 * value * value) * INV_ROOT_TWO_PI


def local(tokens, left_factor, right_factor, cotangent):
    row_count = tokens.shape[0]
    local_blocks = left_factor.shape[0]
    block_size = left_factor.shape[1]
    local_units = right_factor.shape[0]
    all_blocks = right_factor.shape[1]
    blocked = tokens.reshape(row_count, local_blocks, block_size)
    preact = jnp.einsum("tba,baj->tbj", blocked, left_factor, preferred_element_type=jnp.float32)
    activated = gelu_exact(preact).astype(jnp.bfloat16)
    mixed = jnp.einsum(
        "tbj,jbk->tjk",
        lax.all_to_all(activated, "feat", split_axis=2, concat_axis=1, tiled=True),
        right_factor,
        preferred_element_type=jnp.float32,
    ).astype(jnp.bfloat16)
    upstream = cotangent.reshape(row_count, local_units, all_blocks)
    returned = jnp.einsum(
        "tjk,jbk->tbj", upstream, right_factor, preferred_element_type=jnp.float32
    ).astype(jnp.bfloat16)
    gathered = lax.all_to_all(activated, "feat", split_axis=2, concat_axis=1, tiled=True)
    right_grad = jnp.einsum("tbj,tjk->jbk", gathered, upstream, preferred_element_type=jnp.float32)
    received = lax.all_to_all(returned, "feat", split_axis=1, concat_axis=2, tiled=True)
    preact_grad = (received.astype(jnp.float32) * gelu_slope(preact)).astype(jnp.bfloat16)
    input_grad = jnp.einsum(
        "tbj,baj->tba", preact_grad, left_factor, preferred_element_type=jnp.float32
    ).astype(jnp.bfloat16)
    left_grad = jnp.einsum("tba,tbj->baj", blocked, preact_grad, preferred_element_type=jnp.float32)
    left_grad, right_grad = lax.psum((left_grad, right_grad), "dp")
    norm_factor = 1.0 / math.sqrt(row_count * lax.axis_size("dp"))
    return (
        mixed.reshape(row_count, local_units * all_blocks),
        input_grad.reshape(row_count, local_blocks * block_size),
        left_grad * norm_factor,
        right_grad * norm_factor,
    )


def solution(mesh):
    in_specs = (P("dp", "feat"), P("feat", None, None), P("feat", None, None), P("dp", "feat"))
    out_specs = (P("dp", "feat"), P("dp", "feat"), P("feat", None, None), P("feat", None, None))
    return jax.shard_map(local, mesh=mesh, in_specs=in_specs, out_specs=out_specs, check_vma=False)
```

profile of v0, /device:TPU:1, one launch (start us, length us, event | category | flops | bytes accessed | tf_op | source)
XLA Modules:
  0.0 269.6 jit_solution(9998977184158105321)
XLA Ops:
  7.2 0.0 copy-start
  7.2 3.9 %convert_bitcast_fusion = bf16[1024,256,8]{0,1,2:T(8,128)(2,1)S(1)} fusion(bf16[8,256,256]{2,1,0:T(8,128)(2,1)} %param.6, bf16[128,8,8,256]{3,2,1,0:T(8,128)(2,1)} %bitcast.64), kind=kOutput, calls=%fused_computation.21 | convolution fusion | flops 1075838976 | bytes 9437184 | tf_op jit(solution)/shard_map/tjk,jbk->tbj/dot_general | solution.py:37
  11.1 2.3 copy.64
  13.4 0.0 copy-start.4
  13.4 58.7 %all_to_all.32 = bf16[1024,256,8]{0,2,1:T(8,128)(2,1)S(1)} all-to-all(bf16[1024,256,8]{0,2,1:T(8,128)(2,1)S(1)} %copy.64), channel_id=1, replica_groups=mesh['dp'=4,'feat'=32] {'feat'}, dimensions={1} | all-to-all | bytes 8388608 | tf_op jit(solution)/shard_map/all_to_all | solution.py:42
  72.2 0.0 copy-done
  72.2 0.0 copy-done.4
  72.2 6.4 %fusion.5 = (bf16[1024,8,256]{0,2,1:T(8,128)(2,1)}, bf16[1024,8,256]{0,2,1:T(8,128)(2,1)S(1)}) fusion(bf16[8,256,256]{2,1,0:T(8,128)(2,1)S(1)} %copy-done, bf16[128,8,8,256]{3,2,1,0:T(8,128)(2,1)S(1)} %bitcast.68, bf16[1024,32,8,8]{0,3,2,1:T(8,128)(2,1)S(1)} %bitcast.66), kind=kOutput, calls=%fused_computation.6 | convolution fusion | flops 1103101952 | bytes 17825792 | tf_op jit(solution)/shard_map/tba,baj->tbj/dot_general | solution.py:28
  78.6 4.3 %copy.58 = bf16[1024,8,256]{0,1,2:T(8,128)(2,1)} copy(bf16[1024,8,256]{0,2,1:T(8,128)(2,1)S(1)} %get-tuple-element.23) | data formatting | bytes 8388608 | tf_op jit(solution)/shard_map/convert_element_type | solution.py:29
  82.9 5.0 %all-to-all-start = ((bf16[1024,8,256]{0,1,2:T(8,128)(2,1)}), bf16[1024,8,256]{0,1,2:T(8,128)(2,1)}, u32[]{:S(2)}, u32[]{:S(2)}) async-start(bf16[1024,8,256]{0,1,2:T(8,128)(2,1)} %copy.58), calls=%async_computation | async-start | bytes 8388608 | tf_op jit(solution)/shard_map/all_to_all | solution.py:32
  87.9 0.2 all-reduce.3.cloned.1.call-start
  88.1 6.0 %fusion.30 = f32[8,256,256]{1,2,0:T(8,128)} fusion(bf16[1024,8,256]{0,2,1:T(8,128)(2,1)} %get-tuple-element.22, bf16[128,8,8,256]{3,2,1,0:T(8,128)(2,1)} %bitcast.67), kind=kOutput, calls=%fused_computation.31 | convolution fusion | flops 1073741824 | bytes 10485760 | tf_op jit(solution)/shard_map/tba,tbj->baj/dot_general | solution.py:47
  94.2 47.3 %all-to-all-done = bf16[1024,8,256]{0,1,2:T(8,128)(2,1)} async-done(((bf16[1024,8,256]{0,1,2:T(8,128)(2,1)}), bf16[1024,8,256]{0,1,2:T(8,128)(2,1)}, u32[]{:S(2)}, u32[]{:S(2)}) %all-to-all-start) | async-done | bytes 4194336 | tf_op jit(solution)/shard_map/all_to_all | solution.py:32
  141.5 0.0 copy-start.3
  141.5 6.7 %copy.60 = bf16[1024,32,8,8]{0,3,2,1:T(8,128)(2,1)S(1)} copy(bf16[1024,32,8,8]{0,2,3,1:T(8,128)(2,1)} %bitcast.3) | data formatting | bytes 8388608 | tf_op jit(solution)/shard_map/all_to_all | solution.py:32
  148.2 0.0 copy-start.1
  148.2 2.0 copy-done.1
  150.2 0.0 copy-done.3
  150.2 6.4 %fusion.10 = f32[8,256,256]{1,2,0:T(8,128)} fusion(bf16[128,8,8,256]{3,2,1,0:T(8,128)(2,1)S(1)} %bitcast.65, bf16[1024,256,8]{0,2,1:T(8,128)(2,1)S(1)} %bitcast.60), kind=kOutput, calls=%fused_computation.13 | convolution fusion | flops 1073741824 | bytes 10485760 | tf_op jit(solution)/shard_map/tbj,tjk->jbk/dot_general | solution.py:41
  156.6 0.0 all-reduce.3.cloned.1.call-update
  156.7 5.6 %convolution_convert_fusion = bf16[8,1024,256]{1,2,0:T(8,128)(2,1)} fusion(bf16[8,256,256]{2,1,0:T(8,128)(2,1)S(1)} %copy-done, bf16[1024,8,256]{0,2,1:T(8,128)(2,1)} %get-tuple-element.22), kind=kOutput, calls=%fused_computation.30 | convolution fusion | flops 1075838976 | bytes 9437184 | tf_op jit(solution)/shard_map/tbj,baj->tba/dot_general | solution.py:44
  162.3 0.0 copy-start.2
  162.3 6.5 %copy.72 = bf16[1024,2048]{1,0:T(8,128)(2,1)} copy(bf16[1024,2048]{0,1:T(8,128)(2,1)} %bitcast.62) | data formatting | bytes 8388608
  168.8 0.0 copy-done.2
  168.8 9.8 %fusion.25 = bf16[8,1024,256]{1,2,0:T(8,128)(2,1)} fusion(bf16[8,256,256]{2,1,0:T(8,128)(2,1)S(1)} %copy-done.2, bf16[1024,256,8]{0,2,1:T(8,128)(2,1)} %bitcast.61), kind=kOutput, calls=%fused_computation.29 | convolution fusion | flops 1075838976 | bytes 9437184 | tf_op jit(solution)/shard_map/tbj,jbk->tjk/dot_general | solution.py:30
  178.7 6.4 %copy.71 = bf16[1024,2048]{1,0:T(8,128)(2,1)} copy(bf16[1024,2048]{0,1:T(8,128)(2,1)} %bitcast.63) | data formatting | bytes 8388608
  185.1 69.0 %all-reduce.3.cloned.1.call-done = (f32[8,256,256]{1,2,0:T(8,128)}, f32[8,256,256]{1,2,0:T(8,128)}) async-done(((f32[8,256,256]{1,2,0:T(8,128)}, f32[8,256,256]{1,2,0:T(8,128)}), (f32[8,256,256]{1,2,0:T(8,128)}, f32[8,256,256]{1,2,0:T(8,128)})) %all-reduce.3.cloned.1.call-update) | async-done | bytes 4194320 | tf_op jit(solution)/shard_map/psum | solution.py:48
  254.1 4.0 %broadcast_multiply_fusion = (f32[8,256,256]{1,2,0:T(8,128)}, f32[8,256,256]{1,2,0:T(8,128)S(1)}) fusion(f32[8,256,256]{1,2,0:T(8,128)} %get-tuple-element.21, f32[8,256,256]{1,2,0:T(8,128)} %get-tuple-element.20), kind=kLoop, calls=%fused_computation.32 | loop fusion | flops 1048576 | bytes 8388608 | tf_op jit(solution)/shard_map/mul | solution.py:54
  258.0 2.9 %copy.74 = f32[8,256,256]{2,1,0:T(8,128)} copy(f32[8,256,256]{1,2,0:T(8,128)} %get-tuple-element.24) | data formatting | bytes 4194304
  260.9 1.8 copy.73
Async XLA Ops:
  7.2 65.0 %copy-start = (bf16[8,256,256]{2,1,0:T(8,128)(2,1)S(1)}, bf16[8,256,256]{2,1,0:T(8,128)(2,1)}, u32[]{:S(2)}) copy-start(bf16[8,256,256]{2,1,0:T(8,128)(2,1)} %param.5) | copy-start | bytes 3145732
  13.4 58.8 %copy-start.4 = (bf16[1024,2048]{1,0:T(8,128)(2,1)S(1)}, bf16[1024,2048]{1,0:T(8,128)(2,1)}, u32[]{:S(2)}) copy-start(bf16[1024,2048]{1,0:T(8,128)(2,1)} %param.4) | copy-start | bytes 12582916
  82.9 58.6 %all-to-all-start = ((bf16[1024,8,256]{0,1,2:T(8,128)(2,1)}), bf16[1024,8,256]{0,1,2:T(8,128)(2,1)}, u32[]{:S(2)}, u32[]{:S(2)}) async-start(bf16[1024,8,256]{0,1,2:T(8,128)(2,1)} %copy.58), calls=%async_computation | async-start | bytes 8388608 | tf_op jit(solution)/shard_map/all_to_all | solution.py:32
  87.9 166.2 %all-reduce.3.cloned.1.call-start = ((), (), s32[]{:S(2)}) async-start(), calls=%async_computation.2 | async-start | bytes 8388608 | tf_op jit(solution)/shard_map/psum | solution.py:48
  141.5 8.7 %copy-start.3 = (bf16[1024,2048]{1,0:T(8,128)(2,1)S(1)}, bf16[1024,2048]{1,0:T(8,128)(2,1)}, u32[]{:S(2)}) copy-start(bf16[1024,2048]{1,0:T(8,128)(2,1)} %param.7) | copy-start | bytes 12582916
  148.2 2.0 copy-start.1
  162.3 6.5 %copy-start.2 = (bf16[8,256,256]{2,1,0:T(8,128)(2,1)S(1)}, bf16[8,256,256]{2,1,0:T(8,128)(2,1)}, u32[]{:S(2)}) copy-start(bf16[8,256,256]{2,1,0:T(8,128)(2,1)} %param.6) | copy-start | bytes 3145732
Sparse Core Ops, SparseCore 0:
  156.8 97.2 all-reduce.2
where the time goes:
time: 270 us
  waiting for transfers between devices  116 us (43%)
  blocking collectives  58.7 us (22%)
  matrix products  38.2 us (14%)
  local copies, waits for them, and re-layouts  33 us (12%)
  between operations  14.1 us (5%)
  starting transfers between devices  5.2 us (2%)
  other arithmetic  3.96 us (1%)
    psum x1, waiting for transfers between devices, local(): left_grad, right_grad = lax.psum((left_grad, right_grad), 'dp')  69 us
    all_to_all x1, blocking collectives, local(): lax.all_to_all(returned, 'feat', split_axis=1, concat_axis=2, tiled=True)  58.7 us
    all_to_all x1, waiting for transfers between devices, local(): lax.all_to_all(activated, 'feat', split_axis=2, concat_axis=1, tiled=True)  47.3 us
    unnamed x14, local copies, waits for them, and re-layouts  19.6 us
    dot_general x1, matrix products, local(): jnp.einsum('tbj,jbk->tjk', lax.all_to_all(activated, 'feat', split_axis=2...  9.81 us
    all_to_all x1, local copies, waits for them, and re-layouts, local(): lax.all_to_all(activated, 'feat', split_axis=2, concat_axis=1, tiled=True)  6.69 us
    dot_general x1, matrix products, local(): jnp.einsum('tba,baj->tbj', blocked, left_factor, preferred_element_type=j...  6.41 us
    dot_general x1, matrix products, local(): jnp.einsum('tbj,tjk->jbk', gathered, upstream, preferred_element_type=jnp...  6.4 us
  transfers between devices with their start and end apart: 2, of which 2 were waited for; matrix products, arithmetic and copies ran while one was open for 13% of the time, Pallas kernels for 0%

commit v1 on v0

v1 whole, which is shorter than its diff:
```python
import math

import jax
import jax.numpy as jnp
from jax import lax
from jax.experimental import pallas as pl
from jax.experimental.pallas import tpu as pltpu
from jax.sharding import PartitionSpec as P

SQRT_HALF = 0.7071067811865476
INV_ROOT_TWO_PI = 0.3989422804014327
MESH = pl.DeviceIdType.MESH
F32 = jnp.float32
BF16 = jnp.bfloat16
NT = (((1,), (1,)), ((), ()))
TN = (((0,), (0,)), ((), ()))
TT = (((0,), (1,)), ((), ()))
NF = 32
NB = 8
T = 1024
W = 256
H = 128
ORDER = [(13 * k) % NF for k in range(1, NF)]


def dot(a, b, dims=(((1,), (0,)), ((), ()))):
    return lax.dot_general(a, b, dims, preferred_element_type=F32)


def kernel(
    tok, lf, rf, ct, out, ig, lg, rg,
    x_v, c_v, l_v, r_v, send_d, recv_d, pre_v, send_a, recv_a, out_v, ig_v,
    keep_v, s1_v, r1_v, s2_v, r2_v, grad_v,
    x_sem, c_sem, w_sem, sd_sem, rd_sem, sa_sem, ra_sem, out_sem, ig_sem,
    s1_sem, r1_sem, s2_sem, r2_sem, s3_sem, r3_sem, g_sem,
):
    dp = lax.axis_index("dp")
    me = lax.axis_index("feat")
    core = dp % 2
    sibling = (dp + 1 - 2 * core, me)
    across = ((dp + 2) % 4, me)
    my, mx, mz = me // 16, (me // 4) % 4, me % 4
    peers = [
        ((my + p // 16) % 2) * 16 + ((mx + (p // 4) % 4) % 4) * 4 + (mz + p % 4) % 4 for p in ORDER
    ]

    def cols(n):
        return pl.ds(pl.multiple_of(n * W, W), W)

    pltpu.make_async_copy(rf, r_v, w_sem.at[0]).start()

    @pl.loop(0, NB)
    def _(n):
        pltpu.make_async_copy(ct.at[:, cols(n)], c_v.at[n], c_sem.at[n]).start()

    pltpu.make_async_copy(lf, l_v, w_sem.at[1]).start()

    @pl.loop(0, NB)
    def _(n):
        pltpu.make_async_copy(tok.at[:, cols(n)], x_v.at[n], x_sem.at[n]).start()

    barrier = pltpu.get_barrier_semaphore()
    for p in peers:
        pl.semaphore_signal(barrier, inc=1, device_id=(dp, p), device_id_type=MESH)
    for d in (sibling, across):
        pl.semaphore_signal(barrier, inc=1, device_id=d, device_id_type=MESH)

    def compute_d(i):
        pltpu.make_async_copy(ct.at[:, cols(i)], c_v.at[i], c_sem.at[i]).wait()
        v = dot(r_v[i], c_v[i], NT)
        send_d[i] = v.reshape(NF, NB, T).astype(BF16)

    pltpu.make_async_copy(rf, r_v, w_sem.at[0]).wait()
    compute_d(0)
    pl.semaphore_wait(barrier, NF + 1)

    @pl.loop(0, NB)
    def _(i):
        for p in peers:
            pltpu.make_async_remote_copy(
                src_ref=send_d.at[i, p], dst_ref=recv_d.at[me * NB + i],
                send_sem=sd_sem.at[i], recv_sem=rd_sem.at[i],
                device_id=(dp, p), device_id_type=MESH,
            ).start()
        pltpu.make_async_copy(send_d.at[i, me], recv_d.at[me * NB + i], rd_sem.at[i]).start()

        @pl.when(i < NB - 1)
        def _():
            compute_d(i + 1)

    pltpu.make_async_copy(lf, l_v, w_sem.at[1]).wait()

    @pl.loop(0, NB)
    def _(b):
        pltpu.make_async_copy(tok.at[:, cols(b)], x_v.at[b], x_sem.at[b]).wait()
        v = dot(l_v[b], x_v[b], TT)
        for q in range(T // H):
            pre_v[q, pl.ds(b, W, stride=NB), :] = v[:, q * H:(q + 1) * H]

    @pl.loop(0, NB)
    def _(i):
        @pl.loop(0, NF)
        def _(d):
            j = d * NB + i
            rows = pl.ds(pl.multiple_of(j * NB, NB), NB)
            for q in range(T // H):
                u = pre_v[q, rows, :]
                half = 0.5 * (1.0 + lax.erf(u * SQRT_HALF))
                send_a[j, :, q * H:(q + 1) * H] = (u * half).astype(BF16)
                pre_v[q, rows, :] = half + u * jnp.exp(-0.5 * u * u) * INV_ROOT_TWO_PI

        for p in peers:
            pltpu.make_async_remote_copy(
                src_ref=send_a.at[p * NB + i], dst_ref=recv_a.at[i, me],
                send_sem=sa_sem.at[i], recv_sem=ra_sem.at[i],
                device_id=(dp, p), device_id_type=MESH,
            ).start()
        pltpu.make_async_copy(send_a.at[me * NB + i], recv_a.at[i, me], ra_sem.at[i]).start()

    mine = pl.ds(pl.multiple_of(core * H, H), H)
    other = pl.ds(pl.multiple_of((1 - core) * H, H), H)

    def hop1(g):
        return pltpu.make_async_remote_copy(
            src_ref=s1_v.at[g], dst_ref=r1_v.at[g], send_sem=s1_sem.at[g], recv_sem=r1_sem.at[g],
            device_id=sibling, device_id_type=MESH)

    def hop2(g):
        return pltpu.make_async_remote_copy(
            src_ref=s2_v.at[g], dst_ref=r2_v.at[g], send_sem=s2_sem.at[g], recv_sem=r2_sem.at[g],
            device_id=across, device_id_type=MESH)

    def hop3(g):
        return pltpu.make_async_remote_copy(
            src_ref=grad_v.at[g, mine], dst_ref=grad_v.at[g, mine], send_sem=s3_sem.at[g], recv_sem=r3_sem.at[g],
            device_id=sibling, device_id_type=MESH)

    def first(g, value):
        keep_v[...] = value
        r2_own = keep_v[mine, :]
        s1_v[g] = keep_v[other, :]
        hop1(g).start()
        grad_v[g, mine] = r2_own

    def second(g):
        hop1(g).wait_recv()
        s2_v[g] = (grad_v[g, mine] + r1_v[g]).astype(BF16)
        hop2(g).start()

    norm = 1.0 / math.sqrt(T * 4)

    def third(g):
        hop2(g).wait_recv()
        grad_v[g, mine] = (s2_v[g].astype(F32) + r2_v[g].astype(F32)) * norm
        hop3(g).start()

    @pl.loop(0, NB)
    def _(i):
        pltpu.make_async_copy(send_d.at[i], send_d.at[i], rd_sem.at[i]).wait()

    @pl.loop(0, NF * NB)
    def _(j):
        rows = pl.ds(pl.multiple_of(j * NB, NB), NB)
        for q in range(T // H):
            pre_v[q, rows, :] = pre_v[q, rows, :] * recv_d[j, :, q * H:(q + 1) * H].astype(F32)

    def put_ig(b):
        return pltpu.make_async_copy(ig_v.at[b % 2], ig.at[:, cols(b)], ig_sem.at[b % 2])

    @pl.loop(0, NB)
    def _(b):
        g = jnp.concatenate(
            [pre_v[q, pl.ds(b, W, stride=NB), :].astype(BF16) for q in range(T // H)], axis=1)

        @pl.when(b >= 2)
        def _():
            put_ig(b - 2).wait()

        ig_v[b % 2] = dot(g, l_v[b], TT).astype(BF16)
        put_ig(b).start()
        first(b, dot(g, x_v[b]).T)

        @pl.when(b >= 1)
        def _():
            second(b - 1)

    for b in range(NB - 2, NB):
        put_ig(b).wait()

    def put_out(i):
        return pltpu.make_async_copy(out_v.at[i % 2], out.at[:, cols(i)], out_sem.at[i % 2])

    @pl.loop(0, NB)
    def _(i):
        pltpu.make_async_copy(send_d.at[i], send_d.at[i], ra_sem.at[i]).wait()
        a = recv_a[i].astype(F32).reshape(W, T).astype(BF16)
        first(NB + i, dot(a, c_v[i]))

        @pl.when(i >= 2)
        def _():
            put_out(i - 2).wait()

        out_v[i % 2] = dot(a, r_v[i], TN).astype(BF16)
        put_out(i).start()
        second(NB + i - 1)
        third(i)

        @pl.when(i >= 2)
        def _():
            third(NB + i - 2)

    second(2 * NB - 1)
    third(2 * NB - 2)
    third(2 * NB - 1)

    for b in range(NB - 2, NB):
        put_out(b).wait()

    @pl.loop(0, 2 * NB)
    def _(g):
        hop3(g).wait_recv()
        hop1(g).wait_send()
        hop2(g).wait_send()
        hop3(g).wait_send()

    @pl.loop(0, NB)
    def _(i):
        pltpu.make_async_remote_copy(
            src_ref=send_d.at[i, pl.ds(0, NF - 1)], dst_ref=recv_d.at[pl.ds(0, NF - 1)],
            send_sem=sd_sem.at[i], recv_sem=rd_sem.at[i], device_id=sibling, device_id_type=MESH).wait_send()
        pltpu.make_async_remote_copy(
            src_ref=send_d.at[i, pl.ds(0, NF - 1)], dst_ref=recv_d.at[pl.ds(0, NF - 1)],
            send_sem=sa_sem.at[i], recv_sem=ra_sem.at[i], device_id=sibling, device_id_type=MESH).wait_send()

    a = pltpu.make_async_copy(grad_v.at[pl.ds(0, NB)], lg, g_sem.at[0])
    b = pltpu.make_async_copy(grad_v.at[pl.ds(NB, NB)], rg, g_sem.at[1])
    a.start()
    b.start()
    a.wait()
    b.wait()


def local(tokens, left_factor, right_factor, cotangent):
    any_spec = pl.BlockSpec(memory_space=pl.ANY)
    dma = pltpu.SemaphoreType.DMA
    return pl.pallas_call(
        kernel,
        out_shape=(
            jax.ShapeDtypeStruct(tokens.shape, BF16),
            jax.ShapeDtypeStruct(tokens.shape, BF16),
            jax.ShapeDtypeStruct(left_factor.shape, F32),
            jax.ShapeDtypeStruct(right_factor.shape, F32),
        ),
        in_specs=[any_spec] * 4,
        out_specs=(any_spec,) * 4,
        scratch_shapes=[
            pltpu.VMEM((NB, T, W), BF16), pltpu.VMEM((NB, T, W), BF16),
            pltpu.VMEM((NB, W, W), BF16), pltpu.VMEM((NB, W, W), BF16),
            pltpu.VMEM((NB, NF, NB, T), BF16), pltpu.VMEM((NF * NB, NB, T), BF16),
            pltpu.VMEM((T // H, W * NB, H), F32),
            pltpu.VMEM((NF * NB, NB, T), BF16), pltpu.VMEM((NB, NF, NB, T), BF16),
            pltpu.VMEM((2, T, W), BF16), pltpu.VMEM((2, T, W), BF16),
            pltpu.VMEM((W, W), F32),
            pltpu.VMEM((2 * NB, H, W), F32), pltpu.VMEM((2 * NB, H, W), F32),
            pltpu.VMEM((2 * NB, H, W), BF16), pltpu.VMEM((2 * NB, H, W), BF16),
            pltpu.VMEM((2 * NB, W, W), F32),
            dma((NB,)), dma((NB,)), dma((2,)), dma((NB,)), dma((NB,)), dma((NB,)), dma((NB,)), dma((2,)), dma((2,)),
            dma((2 * NB,)), dma((2 * NB,)), dma((2 * NB,)), dma((2 * NB,)), dma((2 * NB,)), dma((2 * NB,)), dma((2,)),
        ],
        compiler_params=pltpu.CompilerParams(
            collective_id=0, has_side_effects=True, vmem_limit_bytes=63 << 20),
        name="monarch",
    )(tokens, left_factor, right_factor, cotangent)


def solution(mesh):
    in_specs = (P("dp", "feat"), P("feat", None, None), P("feat", None, None), P("dp", "feat"))
    out_specs = (P("dp", "feat"), P("dp", "feat"), P("feat", None, None), P("feat", None, None))
    return jax.shard_map(local, mesh=mesh, in_specs=in_specs, out_specs=out_specs, check_vma=False)
```

time: 270 us -> 149 us (0.55)
  Pallas kernels: 0 us -> 137 us
  waiting for transfers between devices: 116 us -> 0 us
  blocking collectives: 58.7 us -> 0 us
  matrix products: 38.2 us -> 0 us
  local copies, waits for them, and re-layouts: 33 us -> 11.7 us
  between operations: 14.1 us -> 0.65 us
  starting transfers between devices: 5.2 us -> 0 us
  other arithmetic: 3.96 us -> 0 us
    pallas_call x0 -> x1, Pallas kernels: none -> 137 us  [local(): pl.pallas_call(kernel, out_shape=(jax.ShapeDtypeStruct(tokens.shape, BF16...]
    psum x1 -> x0, waiting for transfers between devices: 69 us -> none  [local(): left_grad, right_grad = lax.psum((left_grad, right_grad), 'dp')]
    all_to_all x1 -> x0, blocking collectives: 58.7 us -> none  [local(): lax.all_to_all(returned, 'feat', split_axis=1, concat_axis=2, tiled=True)]
    all_to_all x1 -> x0, waiting for transfers between devices: 47.3 us -> none  [local(): lax.all_to_all(activated, 'feat', split_axis=2, concat_axis=1, tiled=True)]
    dot_general x6 -> x0, matrix products: 38.2 us -> none  [the longest x1 9.81 us: local(): jnp.einsum('tbj,jbk->tjk', lax.all_to_all(activated, 'feat', split_axis=2...]
    unnamed x14 -> x10, local copies, waits for them, and re-layouts: 19.6 us -> 11.7 us
    all_to_all x1 -> x0, local copies, waits for them, and re-layouts: 6.69 us -> none  [local(): lax.all_to_all(activated, 'feat', split_axis=2, concat_axis=1, tiled=True)]
    convert_element_type x2 -> x0, local copies, waits for them, and re-layouts: 6.66 us -> none  [the longest x1 4.33 us: local(): activated = gelu_exact(preact).astype(jnp.bfloat16)]
  transfers between devices with their start and end apart: 2 -> 0, of which waited for: 2 -> 0; matrix products, arithmetic and copies ran while one was open for 13% -> 0% of each run, Pallas kernels for 0% -> 0%
where the time goes in v1:
time: 149 us
  Pallas kernels  137 us (92%)
  local copies, waits for them, and re-layouts  11.7 us (8%)
    pallas_call x1, Pallas kernels, local(): pl.pallas_call(kernel, out_shape=(jax.ShapeDtypeStruct(tokens.shape, BF16...  137 us
    unnamed x10, local copies, waits for them, and re-layouts  11.7 us

profile of v1, /device:TPU:1, one launch (start us, length us, event | category | flops | bytes accessed | tf_op | source)
XLA Modules:
  0.0 148.9 jit_solution(12508451119721068788)
XLA Ops:
  0.6 136.6 %monarch.1 = (bf16[1024,2048]{1,0:T(8,128)(2,1)}, bf16[1024,2048]{1,0:T(8,128)(2,1)}, f32[8,256,256]{2,1,0:T(8,128)}, f32[8,256,256]{2,1,0:T(8,128)}) custom-call(bf16[1024,2048]{1,0:T(8,128)(2,1)} %tok.1, bf16[8,256,256]{2,1,0:T(8,128)(2,1)} %lf.1, bf16[8,256,256]{2,1,0:T(8,128)(2,1)} %rf.1, bf16[1024,2048]{1,0:T(8,128)(2,1)} %ct.1), custom_call_target="tpu_custom_call" | custom-call | tf_op jit(solution)/shard_map/monarch/pallas_call | solution.py:246
  137.2 0.0 copy-start
  137.2 4.9 %copy.12 = bf16[1024,2048]{1,0:T(8,128)(2,1)} copy(bf16[1024,2048]{1,0:T(8,128)(2,1)} %get-tuple-element.8) | data formatting | bytes 8388608
  142.2 0.0 copy-done
  142.2 0.0 copy-start.2
  142.2 2.1 %copy.13 = bf16[1024,2048]{1,0:T(8,128)(2,1)} copy(bf16[1024,2048]{1,0:T(8,128)(2,1)S(1)} %copy-done) | data formatting | bytes 8388608
  144.3 1.0 copy-done.2
  145.3 0.0 copy-start.1
  145.3 1.3 copy.14
  146.6 1.0 copy-done.1
  147.6 1.3 copy.15
Async XLA Ops:
  137.2 5.0 %copy-start = (bf16[1024,2048]{1,0:T(8,128)(2,1)S(1)}, bf16[1024,2048]{1,0:T(8,128)(2,1)}, u32[]{:S(2)}) copy-start(bf16[1024,2048]{1,0:T(8,128)(2,1)} %get-tuple-element.9) | copy-start | bytes 12582916
  142.2 3.1 %copy-start.2 = (f32[8,256,256]{2,1,0:T(8,128)S(1)}, f32[8,256,256]{2,1,0:T(8,128)}, u32[]{:S(2)}) copy-start(f32[8,256,256]{2,1,0:T(8,128)} %get-tuple-element.10) | copy-start | bytes 6291460
  145.3 2.3 %copy-start.1 = (f32[8,256,256]{2,1,0:T(8,128)S(1)}, f32[8,256,256]{2,1,0:T(8,128)}, u32[]{:S(2)}) copy-start(f32[8,256,256]{2,1,0:T(8,128)} %get-tuple-element.11) | copy-start | bytes 6291460

commit v2 on v1

--- a/solution.py
+++ b/solution.py
@@ -20,7 +20,7 @@
 T = 1024
 W = 256
 H = 128
-ORDER = [(13 * k) % NF for k in range(1, NF)]
+ORDER = sorted([(13 * k) % NF for k in range(1, NF)], key=lambda p: p < NF // 2)
 
 
 def dot(a, b, dims=(((1,), (0,)), ((), ()))):
@@ -28,11 +28,11 @@
 
 
 def kernel(
-    tok, lf, rf, ct, out, ig, lg, rg,
-    x_v, c_v, l_v, r_v, send_d, recv_d, pre_v, send_a, recv_a, out_v, ig_v,
-    keep_v, s1_v, r1_v, s2_v, r2_v, grad_v,
-    x_sem, c_sem, w_sem, sd_sem, rd_sem, sa_sem, ra_sem, out_sem, ig_sem,
-    s1_sem, r1_sem, s2_sem, r2_sem, s3_sem, r3_sem, g_sem,
+    tok, lf, rf, ct, c_v, x_v, grad_v,
+    l_v, r_v, send_d, recv_d, pre_v, send_a, recv_a,
+    keep_v, s1_v, r1_v, s2_v, r2_v,
+    x_sem, c_sem, w_sem, sd_sem, rd_sem, sa_sem, ra_sem,
+    s1_sem, r1_sem, s2_sem, r2_sem, s3_sem, r3_sem,
 ):
     dp = lax.axis_index("dp")
     me = lax.axis_index("feat")
@@ -97,6 +97,15 @@
         for q in range(T // H):
             pre_v[q, pl.ds(b, W, stride=NB), :] = v[:, q * H:(q + 1) * H]
 
+    def push_a(i):
+        for p in peers:
+            pltpu.make_async_remote_copy(
+                src_ref=send_a.at[p * NB + i], dst_ref=recv_a.at[i, me],
+                send_sem=sa_sem.at[i], recv_sem=ra_sem.at[i],
+                device_id=(dp, p), device_id_type=MESH,
+            ).start()
+        pltpu.make_async_copy(send_a.at[me * NB + i], recv_a.at[i, me], ra_sem.at[i]).start()
+
     @pl.loop(0, NB)
     def _(i):
         @pl.loop(0, NF)
@@ -109,13 +118,7 @@
                 send_a[j, :, q * H:(q + 1) * H] = (u * half).astype(BF16)
                 pre_v[q, rows, :] = half + u * jnp.exp(-0.5 * u * u) * INV_ROOT_TWO_PI
 
-        for p in peers:
-            pltpu.make_async_remote_copy(
-                src_ref=send_a.at[p * NB + i], dst_ref=recv_a.at[i, me],
-                send_sem=sa_sem.at[i], recv_sem=ra_sem.at[i],
-                device_id=(dp, p), device_id_type=MESH,
-            ).start()
-        pltpu.make_async_copy(send_a.at[me * NB + i], recv_a.at[i, me], ra_sem.at[i]).start()
+        push_a(i)
 
     mine = pl.ds(pl.multiple_of(core * H, H), H)
     other = pl.ds(pl.multiple_of((1 - core) * H, H), H)
@@ -158,63 +161,37 @@
     def _(i):
         pltpu.make_async_copy(send_d.at[i], send_d.at[i], rd_sem.at[i]).wait()
 
-    @pl.loop(0, NF * NB)
-    def _(j):
-        rows = pl.ds(pl.multiple_of(j * NB, NB), NB)
-        for q in range(T // H):
-            pre_v[q, rows, :] = pre_v[q, rows, :] * recv_d[j, :, q * H:(q + 1) * H].astype(F32)
-
-    def put_ig(b):
-        return pltpu.make_async_copy(ig_v.at[b % 2], ig.at[:, cols(b)], ig_sem.at[b % 2])
+        @pl.loop(0, NF)
+        def _(d):
+            j = d * NB + i
+            rows = pl.ds(pl.multiple_of(j * NB, NB), NB)
+            for q in range(T // H):
+                pre_v[q, rows, :] = pre_v[q, rows, :] * recv_d[j, :, q * H:(q + 1) * H].astype(F32)
 
     @pl.loop(0, NB)
     def _(b):
         g = jnp.concatenate(
             [pre_v[q, pl.ds(b, W, stride=NB), :].astype(BF16) for q in range(T // H)], axis=1)
-
-        @pl.when(b >= 2)
-        def _():
-            put_ig(b - 2).wait()
-
-        ig_v[b % 2] = dot(g, l_v[b], TT).astype(BF16)
-        put_ig(b).start()
         first(b, dot(g, x_v[b]).T)
+        x_v[b] = dot(g, l_v[b], TT).astype(BF16)
 
         @pl.when(b >= 1)
         def _():
             second(b - 1)
 
-    for b in range(NB - 2, NB):
-        put_ig(b).wait()
-
-    def put_out(i):
-        return pltpu.make_async_copy(out_v.at[i % 2], out.at[:, cols(i)], out_sem.at[i % 2])
-
     @pl.loop(0, NB)
     def _(i):
         pltpu.make_async_copy(send_d.at[i], send_d.at[i], ra_sem.at[i]).wait()
         a = recv_a[i].astype(F32).reshape(W, T).astype(BF16)
         first(NB + i, dot(a, c_v[i]))
-
-        @pl.when(i >= 2)
-        def _():
-            put_out(i - 2).wait()
-
-        out_v[i % 2] = dot(a, r_v[i], TN).astype(BF16)
-        put_out(i).start()
+        c_v[i] = dot(a, r_v[i], TN).astype(BF16)
         second(NB + i - 1)
-        third(i)
-
-        @pl.when(i >= 2)
-        def _():
-            third(NB + i - 2)
 
     second(2 * NB - 1)
-    third(2 * NB - 2)
-    third(2 * NB - 1)
-
-    for b in range(NB - 2, NB):
-        put_out(b).wait()
+
+    @pl.loop(0, 2 * NB)
+    def _(g):
+        third(g)
 
     @pl.loop(0, 2 * NB)
     def _(g):
@@ -232,45 +209,63 @@
             src_ref=send_d.at[i, pl.ds(0, NF - 1)], dst_ref=recv_d.at[pl.ds(0, NF - 1)],
             send_sem=sa_sem.at[i], recv_sem=ra_sem.at[i], device_id=sibling, device_id_type=MESH).wait_send()
 
-    a = pltpu.make_async_copy(grad_v.at[pl.ds(0, NB)], lg, g_sem.at[0])
-    b = pltpu.make_async_copy(grad_v.at[pl.ds(NB, NB)], rg, g_sem.at[1])
-    a.start()
-    b.start()
-    a.wait()
-    b.wait()
+
+def write(out_v, ig_v, grad_v, out, ig, lg, rg, sem):
+    copies = [
+        pltpu.make_async_copy(grad_v.at[pl.ds(0, NB)], lg, sem.at[0]),
+        pltpu.make_async_copy(grad_v.at[pl.ds(NB, NB)], rg, sem.at[1]),
+    ]
+    for n in range(NB):
+        copies.append(pltpu.make_async_copy(out_v.at[n], out.at[:, n * W:(n + 1) * W], sem.at[2 + n]))
+        copies.append(pltpu.make_async_copy(ig_v.at[n], ig.at[:, n * W:(n + 1) * W], sem.at[2 + NB + n]))
+    for copy in copies:
+        copy.start()
+    for copy in copies:
+        copy.wait()
 
 
 def local(tokens, left_factor, right_factor, cotangent):
     any_spec = pl.BlockSpec(memory_space=pl.ANY)
     dma = pltpu.SemaphoreType.DMA
+    vmem_spec = pl.BlockSpec(memory_space=pltpu.VMEM)
+    held = pl.pallas_call(
+        kernel,
+        out_shape=(
+            jax.ShapeDtypeStruct((NB, T, W), BF16),
+            jax.ShapeDtypeStruct((NB, T, W), BF16),
+            jax.ShapeDtypeStruct((2 * NB, W, W), F32),
+        ),
+        in_specs=[pl.BlockSpec(memory_space=pltpu.HBM)] * 4,
+        out_specs=(vmem_spec,) * 3,
+        scratch_shapes=[
+            pltpu.VMEM((NB, W, W), BF16), pltpu.VMEM((NB, W, W), BF16),
+            pltpu.VMEM((NB, NF, NB, T), BF16), pltpu.VMEM((NF * NB, NB, T), BF16),
+            pltpu.VMEM((T // H, W * NB, H), F32),
+            pltpu.VMEM((NF * NB, NB, T), BF16), pltpu.VMEM((NB, NF, NB, T), BF16),
+            pltpu.VMEM((W, W), F32),
+            pltpu.VMEM((2 * NB, H, W), F32), pltpu.VMEM((2 * NB, H, W), F32),
+            pltpu.VMEM((2 * NB, H, W), BF16), pltpu.VMEM((2 * NB, H, W), BF16),
+            dma((NB,)), dma((NB,)), dma((2,)), dma((NB,)), dma((NB,)), dma((NB,)), dma((NB,)),
+            dma((2 * NB,)), dma((2 * NB,)), dma((2 * NB,)), dma((2 * NB,)), dma((2 * NB,)), dma((2 * NB,)),
+        ],
+        compiler_params=pltpu.CompilerParams(
+            collective_id=0, has_side_effects=True, vmem_limit_bytes=36 << 20),
+        name="monarch",
+    )(*[pltpu.with_memory_space_constraint(v, pltpu.HBM) for v in (tokens, left_factor, right_factor, cotangent)])
     return pl.pallas_call(
-        kernel,
+        write,
         out_shape=(
             jax.ShapeDtypeStruct(tokens.shape, BF16),
             jax.ShapeDtypeStruct(tokens.shape, BF16),
             jax.ShapeDtypeStruct(left_factor.shape, F32),
             jax.ShapeDtypeStruct(right_factor.shape, F32),
         ),
-        in_specs=[any_spec] * 4,
+        in_specs=[vmem_spec] * 3,
         out_specs=(any_spec,) * 4,
-        scratch_shapes=[
-            pltpu.VMEM((NB, T, W), BF16), pltpu.VMEM((NB, T, W), BF16),
-            pltpu.VMEM((NB, W, W), BF16), pltpu.VMEM((NB, W, W), BF16),
-            pltpu.VMEM((NB, NF, NB, T), BF16), pltpu.VMEM((NF * NB, NB, T), BF16),
-            pltpu.VMEM((T // H, W * NB, H), F32),
-            pltpu.VMEM((NF * NB, NB, T), BF16), pltpu.VMEM((NB, NF, NB, T), BF16),
-            pltpu.VMEM((2, T, W), BF16), pltpu.VMEM((2, T, W), BF16),
-            pltpu.VMEM((W, W), F32),
-            pltpu.VMEM((2 * NB, H, W), F32), pltpu.VMEM((2 * NB, H, W), F32),
-            pltpu.VMEM((2 * NB, H, W), BF16), pltpu.VMEM((2 * NB, H, W), BF16),
-            pltpu.VMEM((2 * NB, W, W), F32),
-            dma((NB,)), dma((NB,)), dma((2,)), dma((NB,)), dma((NB,)), dma((NB,)), dma((NB,)), dma((2,)), dma((2,)),
-            dma((2 * NB,)), dma((2 * NB,)), dma((2 * NB,)), dma((2 * NB,)), dma((2 * NB,)), dma((2 * NB,)), dma((2,)),
-        ],
-        compiler_params=pltpu.CompilerParams(
-            collective_id=0, has_side_effects=True, vmem_limit_bytes=63 << 20),
-        name="monarch",
-    )(tokens, left_factor, right_factor, cotangent)
+        scratch_shapes=[dma((2 + 2 * NB,))],
+        compiler_params=pltpu.CompilerParams(vmem_limit_bytes=1 << 20),
+        name="write",
+    )(*held)
 
 
 def solution(mesh):

time: 149 us -> 133 us (0.89)
  local copies, waits for them, and re-layouts: 11.7 us -> 0 us
  Pallas kernels: 137 us -> 132 us
    unnamed x10 -> x0, local copies, waits for them, and re-layouts: 11.7 us -> none
    pallas_call x1 -> x2, Pallas kernels: 137 us -> 132 us  [the longest x1 127 us: local(): pl.pallas_call(kernel, out_shape=(jax.ShapeDtypeStruct((NB, T, W), BF16),...]
where the time goes in v2:
time: 133 us
  Pallas kernels  132 us (99%)
    pallas_call x1, Pallas kernels, local(): pl.pallas_call(kernel, out_shape=(jax.ShapeDtypeStruct((NB, T, W), BF16),...  127 us
    pallas_call x1, Pallas kernels, local(): pl.pallas_call(write, out_shape=(jax.ShapeDtypeStruct(tokens.shape, BF16)...  4.7 us

profile of v2, /device:TPU:1, one launch (start us, length us, event | category | flops | bytes accessed | tf_op | source)
XLA Modules:
  0.0 132.6 jit_solution(18391327235531982952)
XLA Ops:
  0.6 127.3 %monarch.1 = (bf16[8,1024,256]{2,1,0:T(8,128)(2,1)S(1)}, bf16[8,1024,256]{2,1,0:T(8,128)(2,1)S(1)}, f32[16,256,256]{2,1,0:T(8,128)S(1)}) custom-call(bf16[1024,2048]{1,0:T(8,128)(2,1)} %tok.1, bf16[8,256,256]{2,1,0:T(8,128)(2,1)} %lf.1, bf16[8,256,256]{2,1,0:T(8,128)(2,1)} %rf.1, bf16[1024,2048]{1,0:T(8,128)(2,1)} %ct.1), custom_call_target="tpu_custom_call" | custom-call | tf_op jit(solution)/shard_map/monarch/pallas_call | solution.py:231
  127.9 4.7 %write.1 = (bf16[1024,2048]{1,0:T(8,128)(2,1)}, bf16[1024,2048]{1,0:T(8,128)(2,1)}, f32[8,256,256]{2,1,0:T(8,128)}, f32[8,256,256]{2,1,0:T(8,128)}) custom-call(bf16[8,1024,256]{2,1,0:T(8,128)(2,1)S(1)} %get-tuple-element.7.out_v, bf16[8,1024,256]{2,1,0:T(8,128)(2,1)S(1)} %get-tuple-element.8.ig_v, f32[16,256,256]{2,1,0:T(8,128)S(1)} %get-tuple-element.9.grad_v), custom_call_target="tpu_custom_call" | custom-call | tf_op jit(solution)/shard_map/write/pallas_call | solution.py:255

commit v3 on v2

--- a/solution.py
+++ b/solution.py
@@ -16,11 +16,13 @@
 TN = (((0,), (0,)), ((), ()))
 TT = (((0,), (1,)), ((), ()))
 NF = 32
+NP = 16
 NB = 8
 T = 1024
 W = 256
 H = 128
-ORDER = sorted([(13 * k) % NF for k in range(1, NF)], key=lambda p: p < NF // 2)
+ORDER = [(7 * k) % NP for k in range(1, NP)]
+HOLD = 1
 
 
 def dot(a, b, dims=(((1,), (0,)), ((), ()))):
@@ -29,9 +31,9 @@
 
 def kernel(
     tok, lf, rf, ct, c_v, x_v, grad_v,
-    l_v, r_v, send_d, recv_d, pre_v, send_a, recv_a,
+    l_v, r_v, send_d, mid_d, recv_d, pre_v, send_a, mid_a, recv_a,
     keep_v, s1_v, r1_v, s2_v, r2_v,
-    x_sem, c_sem, w_sem, sd_sem, rd_sem, sa_sem, ra_sem,
+    x_sem, c_sem, w_sem, sd_sem, yd_sem, md_sem, rd_sem, sa_sem, ya_sem, ma_sem, ra_sem,
     s1_sem, r1_sem, s2_sem, r2_sem, s3_sem, r3_sem,
 ):
     dp = lax.axis_index("dp")
@@ -39,72 +41,103 @@
     core = dp % 2
     sibling = (dp + 1 - 2 * core, me)
     across = ((dp + 2) % 4, me)
-    my, mx, mz = me // 16, (me // 4) % 4, me % 4
-    peers = [
-        ((my + p // 16) % 2) * 16 + ((mx + (p // 4) % 4) % 4) * 4 + (mz + p % 4) % 4 for p in ORDER
-    ]
+    plane, spot = me // NP, me % NP
+    flip = (1 - plane) * NP + spot
+    peers = [((spot // 4 + p // 4) % 4) * 4 + (spot + p) % 4 for p in ORDER]
 
     def cols(n):
         return pl.ds(pl.multiple_of(n * W, W), W)
 
-    pltpu.make_async_copy(rf, r_v, w_sem.at[0]).start()
-
-    @pl.loop(0, NB)
+    def load_c(n):
+        return pltpu.make_async_copy(ct.at[:, cols(n)], c_v.at[n], c_sem.at[n])
+
+    def load_x(n):
+        return pltpu.make_async_copy(tok.at[:, cols(n)], x_v.at[n], x_sem.at[n])
+
+    load_r0 = pltpu.make_async_copy(rf.at[0], r_v.at[0], w_sem.at[2])
+    load_r = pltpu.make_async_copy(rf.at[pl.ds(1, NB - 1)], r_v.at[pl.ds(1, NB - 1)], w_sem.at[0])
+    load_l = pltpu.make_async_copy(lf, l_v, w_sem.at[1])
+    load_r0.start()
+    load_c(0).start()
+
+    barrier = pltpu.get_barrier_semaphore()
+    for d in [sibling, across, (dp, flip)] + [(dp, plane * NP + p) for p in peers]:
+        pl.semaphore_signal(barrier, inc=1, device_id=d, device_id_type=MESH)
+
+    load_r.start()
+
+    @pl.loop(1, NB)
     def _(n):
-        pltpu.make_async_copy(ct.at[:, cols(n)], c_v.at[n], c_sem.at[n]).start()
-
-    pltpu.make_async_copy(lf, l_v, w_sem.at[1]).start()
+        load_c(n).start()
+
+    load_l.start()
 
     @pl.loop(0, NB)
     def _(n):
-        pltpu.make_async_copy(tok.at[:, cols(n)], x_v.at[n], x_sem.at[n]).start()
-
-    barrier = pltpu.get_barrier_semaphore()
-    for p in peers:
-        pl.semaphore_signal(barrier, inc=1, device_id=(dp, p), device_id_type=MESH)
-    for d in (sibling, across):
-        pl.semaphore_signal(barrier, inc=1, device_id=d, device_id_type=MESH)
+        load_x(n).start()
+
+    def over(i, send, mid, ssem, rsem):
+        return pltpu.make_async_remote_copy(
+            src_ref=send.at[i, pl.ds((1 - plane) * NP, NP)], dst_ref=mid.at[i],
+            send_sem=ssem.at[i], recv_sem=rsem.at[i], device_id=(dp, flip), device_id_type=MESH)
+
+    def spread(src, dst, ssem, rsem):
+        for p in peers:
+            pltpu.make_async_remote_copy(
+                src_ref=src(p), dst_ref=dst, send_sem=ssem, recv_sem=rsem,
+                device_id=(dp, plane * NP + p), device_id_type=MESH).start()
+        pltpu.make_async_copy(src(spot), dst, rsem).start()
+
+    def over_d(i):
+        return over(i, send_d, mid_d, yd_sem, md_sem)
+
+    def own_d(i):
+        spread(lambda p: send_d.at[i, plane * NP + p], recv_d.at[me * NB + i], sd_sem.at[i], rd_sem.at[i])
+
+    def forward_d(i):
+        over_d(i).wait_recv()
+        spread(lambda p: mid_d.at[i, p], recv_d.at[flip * NB + i], sd_sem.at[i], rd_sem.at[i])
+
+    def over_a(i):
+        return over(i, send_a, mid_a, ya_sem, ma_sem)
+
+    def own_a(i):
+        spread(lambda p: send_a.at[i, plane * NP + p], recv_a.at[i, me], sa_sem.at[i], ra_sem.at[i])
+
+    def forward_a(i):
+        over_a(i).wait_recv()
+        spread(lambda p: mid_a.at[i, p], recv_a.at[i, flip], sa_sem.at[i], ra_sem.at[i])
 
     def compute_d(i):
-        pltpu.make_async_copy(ct.at[:, cols(i)], c_v.at[i], c_sem.at[i]).wait()
+        load_c(i).wait()
         v = dot(r_v[i], c_v[i], NT)
         send_d[i] = v.reshape(NF, NB, T).astype(BF16)
 
-    pltpu.make_async_copy(rf, r_v, w_sem.at[0]).wait()
+    load_r0.wait()
     compute_d(0)
-    pl.semaphore_wait(barrier, NF + 1)
-
-    @pl.loop(0, NB)
-    def _(i):
-        for p in peers:
-            pltpu.make_async_remote_copy(
-                src_ref=send_d.at[i, p], dst_ref=recv_d.at[me * NB + i],
-                send_sem=sd_sem.at[i], recv_sem=rd_sem.at[i],
-                device_id=(dp, p), device_id_type=MESH,
-            ).start()
-        pltpu.make_async_copy(send_d.at[i, me], recv_d.at[me * NB + i], rd_sem.at[i]).start()
-
-        @pl.when(i < NB - 1)
-        def _():
-            compute_d(i + 1)
-
-    pltpu.make_async_copy(lf, l_v, w_sem.at[1]).wait()
+    pl.semaphore_wait(barrier, NP + 2)
+    over_d(0).start()
+    own_d(0)
+    load_r.wait()
+
+    @pl.loop(1, NB)
+    def _(i):
+        compute_d(i)
+        over_d(i).start()
+        own_d(i)
+
+    load_l.wait()
 
     @pl.loop(0, NB)
     def _(b):
-        pltpu.make_async_copy(tok.at[:, cols(b)], x_v.at[b], x_sem.at[b]).wait()
+        load_x(b).wait()
         v = dot(l_v[b], x_v[b], TT)
         for q in range(T // H):
             pre_v[q, pl.ds(b, W, stride=NB), :] = v[:, q * H:(q + 1) * H]
 
-    def push_a(i):
-        for p in peers:
-            pltpu.make_async_remote_copy(
-                src_ref=send_a.at[p * NB + i], dst_ref=recv_a.at[i, me],
-                send_sem=sa_sem.at[i], recv_sem=ra_sem.at[i],
-                device_id=(dp, p), device_id_type=MESH,
-            ).start()
-        pltpu.make_async_copy(send_a.at[me * NB + i], recv_a.at[i, me], ra_sem.at[i]).start()
+        @pl.when(b % 2 == 1)
+        def _():
+            forward_d(b // 2)
 
     @pl.loop(0, NB)
     def _(i):
@@ -115,10 +148,15 @@
             for q in range(T // H):
                 u = pre_v[q, rows, :]
                 half = 0.5 * (1.0 + lax.erf(u * SQRT_HALF))
-                send_a[j, :, q * H:(q + 1) * H] = (u * half).astype(BF16)
+                send_a[i, d, :, q * H:(q + 1) * H] = (u * half).astype(BF16)
                 pre_v[q, rows, :] = half + u * jnp.exp(-0.5 * u * u) * INV_ROOT_TWO_PI
 
-        push_a(i)
+        over_a(i).start()
+        own_a(i)
+
+        @pl.when(i % 2 == 1)
+        def _():
+            forward_d(NB // 2 + i // 2)
 
     mine = pl.ds(pl.multiple_of(core * H, H), H)
     other = pl.ds(pl.multiple_of((1 - core) * H, H), H)
@@ -175,9 +213,9 @@
         first(b, dot(g, x_v[b]).T)
         x_v[b] = dot(g, l_v[b], TT).astype(BF16)
 
-        @pl.when(b >= 1)
-        def _():
-            second(b - 1)
+        @pl.when(b % 2 == 1)
+        def _():
+            forward_a(b // 2)
 
     @pl.loop(0, NB)
     def _(i):
@@ -185,29 +223,43 @@
         a = recv_a[i].astype(F32).reshape(W, T).astype(BF16)
         first(NB + i, dot(a, c_v[i]))
         c_v[i] = dot(a, r_v[i], TN).astype(BF16)
-        second(NB + i - 1)
+
+        @pl.when(i < NB // 2)
+        def _():
+            forward_a(NB // 2 + i)
+
+        @pl.when(i == HOLD)
+        def _():
+            @pl.loop(0, NB + HOLD)
+            def _(g):
+                second(g)
+
+        @pl.when(i > HOLD)
+        def _():
+            second(NB + i - 1)
 
     second(2 * NB - 1)
+
+    @pl.loop(0, NB)
+    def _(i):
+        for over_x, sem in ((over_d, sd_sem), (over_a, sa_sem)):
+            over_x(i).wait_send()
+            pltpu.make_async_remote_copy(
+                src_ref=send_d.at[i, pl.ds(0, NF - 2)], dst_ref=recv_d.at[pl.ds(0, NF - 2)],
+                send_sem=sem.at[i], recv_sem=rd_sem.at[i], device_id=sibling, device_id_type=MESH).wait_send()
 
     @pl.loop(0, 2 * NB)
     def _(g):
+        hop1(g).wait_send()
         third(g)
-
-    @pl.loop(0, 2 * NB)
-    def _(g):
-        hop3(g).wait_recv()
-        hop1(g).wait_send()
         hop2(g).wait_send()
-        hop3(g).wait_send()
-
-    @pl.loop(0, NB)
-    def _(i):
-        pltpu.make_async_remote_copy(
-            src_ref=send_d.at[i, pl.ds(0, NF - 1)], dst_ref=recv_d.at[pl.ds(0, NF - 1)],
-            send_sem=sd_sem.at[i], recv_sem=rd_sem.at[i], device_id=sibling, device_id_type=MESH).wait_send()
-        pltpu.make_async_remote_copy(
-            src_ref=send_d.at[i, pl.ds(0, NF - 1)], dst_ref=recv_d.at[pl.ds(0, NF - 1)],
-            send_sem=sa_sem.at[i], recv_sem=ra_sem.at[i], device_id=sibling, device_id_type=MESH).wait_send()
+
+        @pl.when(g >= 2)
+        def _():
+            hop3(g - 2).wait()
+
+    for g in (2 * NB - 2, 2 * NB - 1):
+        hop3(g).wait()
 
 
 def write(out_v, ig_v, grad_v, out, ig, lg, rg, sem):
@@ -239,17 +291,17 @@
         out_specs=(vmem_spec,) * 3,
         scratch_shapes=[
             pltpu.VMEM((NB, W, W), BF16), pltpu.VMEM((NB, W, W), BF16),
-            pltpu.VMEM((NB, NF, NB, T), BF16), pltpu.VMEM((NF * NB, NB, T), BF16),
+            pltpu.VMEM((NB, NF, NB, T), BF16), pltpu.VMEM((NB, NP, NB, T), BF16), pltpu.VMEM((NF * NB, NB, T), BF16),
             pltpu.VMEM((T // H, W * NB, H), F32),
-            pltpu.VMEM((NF * NB, NB, T), BF16), pltpu.VMEM((NB, NF, NB, T), BF16),
+            pltpu.VMEM((NB, NF, NB, T), BF16), pltpu.VMEM((NB, NP, NB, T), BF16), pltpu.VMEM((NB, NF, NB, T), BF16),
             pltpu.VMEM((W, W), F32),
             pltpu.VMEM((2 * NB, H, W), F32), pltpu.VMEM((2 * NB, H, W), F32),
             pltpu.VMEM((2 * NB, H, W), BF16), pltpu.VMEM((2 * NB, H, W), BF16),
-            dma((NB,)), dma((NB,)), dma((2,)), dma((NB,)), dma((NB,)), dma((NB,)), dma((NB,)),
+            dma((NB,)), dma((NB,)), dma((3,)), *[dma((NB,))] * 8,
             dma((2 * NB,)), dma((2 * NB,)), dma((2 * NB,)), dma((2 * NB,)), dma((2 * NB,)), dma((2 * NB,)),
         ],
         compiler_params=pltpu.CompilerParams(
-            collective_id=0, has_side_effects=True, vmem_limit_bytes=36 << 20),
+            collective_id=0, has_side_effects=True, vmem_limit_bytes=40 << 20),
         name="monarch",
     )(*[pltpu.with_memory_space_constraint(v, pltpu.HBM) for v in (tokens, left_factor, right_factor, cotangent)])
     return pl.pallas_call(

time: 133 us -> 132 us (level)
  no operation moved by 1% of the time
where the time goes in v3:
time: 132 us
  Pallas kernels  131 us (99%)
    pallas_call x1, Pallas kernels, local(): pl.pallas_call(kernel, out_shape=(jax.ShapeDtypeStruct((NB, T, W), BF16),...  127 us
    pallas_call x1, Pallas kernels, local(): pl.pallas_call(write, out_shape=(jax.ShapeDtypeStruct(tokens.shape, BF16)...  4.7 us

profile of v3, /device:TPU:1, one launch (start us, length us, event | category | flops | bytes accessed | tf_op | source)
XLA Modules:
  0.0 132.1 jit_solution(14307004429916716678)
XLA Ops:
  0.6 126.7 %monarch.1 = (bf16[8,1024,256]{2,1,0:T(8,128)(2,1)S(1)}, bf16[8,1024,256]{2,1,0:T(8,128)(2,1)S(1)}, f32[16,256,256]{2,1,0:T(8,128)S(1)}) custom-call(bf16[1024,2048]{1,0:T(8,128)(2,1)} %tok.1, bf16[8,256,256]{2,1,0:T(8,128)(2,1)} %lf.1, bf16[8,256,256]{2,1,0:T(8,128)(2,1)} %rf.1, bf16[1024,2048]{1,0:T(8,128)(2,1)} %ct.1), custom_call_target="tpu_custom_call" | custom-call | tf_op jit(solution)/shard_map/monarch/pallas_call | solution.py:283
  127.4 4.7 %write.1 = (bf16[1024,2048]{1,0:T(8,128)(2,1)}, bf16[1024,2048]{1,0:T(8,128)(2,1)}, f32[8,256,256]{2,1,0:T(8,128)}, f32[8,256,256]{2,1,0:T(8,128)}) custom-call(bf16[8,1024,256]{2,1,0:T(8,128)(2,1)S(1)} %get-tuple-element.7.out_v, bf16[8,1024,256]{2,1,0:T(8,128)(2,1)S(1)} %get-tuple-element.8.ig_v, f32[16,256,256]{2,1,0:T(8,128)S(1)} %get-tuple-element.9.grad_v), custom_call_target="tpu_custom_call" | custom-call | tf_op jit(solution)/shard_map/write/pallas_call | solution.py:307

commit v4 on v3

--- a/solution.py
+++ b/solution.py
@@ -22,7 +22,7 @@
 W = 256
 H = 128
 ORDER = [(7 * k) % NP for k in range(1, NP)]
-HOLD = 1
+LAG = 5
 
 
 def dot(a, b, dims=(((1,), (0,)), ((), ()))):
@@ -228,15 +228,16 @@
         def _():
             forward_a(NB // 2 + i)
 
-        @pl.when(i == HOLD)
-        def _():
-            @pl.loop(0, NB + HOLD)
-            def _(g):
-                second(g)
-
-        @pl.when(i > HOLD)
-        def _():
-            second(NB + i - 1)
+        second(2 * i)
+
+        @pl.when(i < NB - 1)
+        def _():
+            second(2 * i + 1)
+
+        @pl.when(i >= LAG)
+        def _():
+            third(2 * (i - LAG))
+            third(2 * (i - LAG) + 1)
 
     second(2 * NB - 1)
 
@@ -251,14 +252,17 @@
     @pl.loop(0, 2 * NB)
     def _(g):
         hop1(g).wait_send()
+
+    @pl.loop(0, 2 * (NB - LAG))
+    def _(g):
+        hop3(g).wait()
+        hop2(g).wait_send()
+
+    for g in range(2 * (NB - LAG), 2 * NB):
         third(g)
+
+    for g in range(2 * (NB - LAG), 2 * NB):
         hop2(g).wait_send()
-
-        @pl.when(g >= 2)
-        def _():
-            hop3(g - 2).wait()
-
-    for g in (2 * NB - 2, 2 * NB - 1):
         hop3(g).wait()
 
 

time: 132 us -> 132 us (level)
  no operation moved by 1% of the time
where the time goes in v4:
time: 132 us
  Pallas kernels  131 us (99%)
    pallas_call x1, Pallas kernels, local(): pl.pallas_call(kernel, out_shape=(jax.ShapeDtypeStruct((NB, T, W), BF16),...  127 us
    pallas_call x1, Pallas kernels, local(): pl.pallas_call(write, out_shape=(jax.ShapeDtypeStruct(tokens.shape, BF16)...  4.7 us

profile of v4, /device:TPU:1, one launch (start us, length us, event | category | flops | bytes accessed | tf_op | source)
XLA Modules:
  0.0 132.1 jit_solution(18366431990199297026)
XLA Ops:
  0.6 126.7 %monarch.1 = (bf16[8,1024,256]{2,1,0:T(8,128)(2,1)S(1)}, bf16[8,1024,256]{2,1,0:T(8,128)(2,1)S(1)}, f32[16,256,256]{2,1,0:T(8,128)S(1)}) custom-call(bf16[1024,2048]{1,0:T(8,128)(2,1)} %tok.1, bf16[8,256,256]{2,1,0:T(8,128)(2,1)} %lf.1, bf16[8,256,256]{2,1,0:T(8,128)(2,1)} %rf.1, bf16[1024,2048]{1,0:T(8,128)(2,1)} %ct.1), custom_call_target="tpu_custom_call" | custom-call | tf_op jit(solution)/shard_map/monarch/pallas_call | solution.py:287
  127.4 4.7 %write.1 = (bf16[1024,2048]{1,0:T(8,128)(2,1)}, bf16[1024,2048]{1,0:T(8,128)(2,1)}, f32[8,256,256]{2,1,0:T(8,128)}, f32[8,256,256]{2,1,0:T(8,128)}) custom-call(bf16[8,1024,256]{2,1,0:T(8,128)(2,1)S(1)} %get-tuple-element.7.out_v, bf16[8,1024,256]{2,1,0:T(8,128)(2,1)S(1)} %get-tuple-element.8.ig_v, f32[16,256,256]{2,1,0:T(8,128)S(1)} %get-tuple-element.9.grad_v), custom_call_target="tpu_custom_call" | custom-call | tf_op jit(solution)/shard_map/write/pallas_call | solution.py:311

commit v5 on v4

--- a/solution.py
+++ b/solution.py
@@ -229,17 +229,12 @@
             forward_a(NB // 2 + i)
 
         second(2 * i)
-
-        @pl.when(i < NB - 1)
-        def _():
-            second(2 * i + 1)
+        second(2 * i + 1)
 
         @pl.when(i >= LAG)
         def _():
             third(2 * (i - LAG))
             third(2 * (i - LAG) + 1)
-
-    second(2 * NB - 1)
 
     @pl.loop(0, NB)
     def _(i):

time: 132 us -> 132 us (level)
  no operation moved by 1% of the time
where the time goes in v5:
time: 132 us
  Pallas kernels  131 us (99%)
    pallas_call x1, Pallas kernels, local(): pl.pallas_call(kernel, out_shape=(jax.ShapeDtypeStruct((NB, T, W), BF16),...  127 us
    pallas_call x1, Pallas kernels, local(): pl.pallas_call(write, out_shape=(jax.ShapeDtypeStruct(tokens.shape, BF16)...  4.7 us

profile of v5, /device:TPU:1, one launch (start us, length us, event | category | flops | bytes accessed | tf_op | source)
XLA Modules:
  0.0 132.1 jit_solution(15505004004861458335)
XLA Ops:
  0.6 126.7 %monarch.1 = (bf16[8,1024,256]{2,1,0:T(8,128)(2,1)S(1)}, bf16[8,1024,256]{2,1,0:T(8,128)(2,1)S(1)}, f32[16,256,256]{2,1,0:T(8,128)S(1)}) custom-call(bf16[1024,2048]{1,0:T(8,128)(2,1)} %tok.1, bf16[8,256,256]{2,1,0:T(8,128)(2,1)} %lf.1, bf16[8,256,256]{2,1,0:T(8,128)(2,1)} %rf.1, bf16[1024,2048]{1,0:T(8,128)(2,1)} %ct.1), custom_call_target="tpu_custom_call" | custom-call | tf_op jit(solution)/shard_map/monarch/pallas_call | solution.py:282
  127.4 4.7 %write.1 = (bf16[1024,2048]{1,0:T(8,128)(2,1)}, bf16[1024,2048]{1,0:T(8,128)(2,1)}, f32[8,256,256]{2,1,0:T(8,128)}, f32[8,256,256]{2,1,0:T(8,128)}) custom-call(bf16[8,1024,256]{2,1,0:T(8,128)(2,1)S(1)} %get-tuple-element.7.out_v, bf16[8,1024,256]{2,1,0:T(8,128)(2,1)S(1)} %get-tuple-element.8.ig_v, f32[16,256,256]{2,1,0:T(8,128)S(1)} %get-tuple-element.9.grad_v), custom_call_target="tpu_custom_call" | custom-call | tf_op jit(solution)/shard_map/write/pallas_call | solution.py:306
